TPU v7x, 32 devices: a whole 2x2x4 slice. The times are simulated.
32 devices in a mesh: space: 8 (over z, x), taxa: 4 (over y, core).
Axes of the slice: x: 2, y: 2, z: 4, core: 2. Of those that a mesh axis runs over, the one named last changes fastest.
Arguments:
- biomass: float32 [2048, 64, 256], P('taxa', 'space'), may hold values from 0.1 to 2
- enzymes: float32 [40, 64, 256], P(None, 'space'), may hold values from 0.1 to 1
- substrates: float32 [12, 64, 256], P(None, 'space'), may hold values from 0.5 to 5
- monomers: float32 [14, 64, 256], P(None, 'space'), may hold values from 0.1 to 2
- enz_traits: int32 [2048, 40], P('taxa'), may hold values 0 or 1
- mono_traits: int32 [2048, 14], P('taxa'), may hold values 0 or 1
- enz_target: int32 [40], replicated, may hold values from 0 to 11
- prod_rate: float32 [2048], P('taxa'), may hold values from 0.002 to 0.02
- uptake_rate: float32 [2048], P('taxa'), may hold values from 0.0005 to 0.005
- mortality: float32 [2048], P('taxa'), may hold values from 0.02 to 0.1
- disperse: float32 [2048], P('taxa'), may hold values from 0.1 to 0.5
- enz_loss: float32 [40], replicated, may hold values from 0.05 to 0.3
- vmax: float32 [40], replicated, may hold values from 0.05 to 0.5
- kmich: float32 [40], replicated, may hold values from 0.5 to 5
- khalf: float32 [14], replicated, may hold values from 0.5 to 5
- offsets: int32 [8, 2], replicated, may hold values from -2 to 2, as said below
Outputs:
- biomass_out: float32 [2048, 64, 256], P('taxa', 'space')
- enzymes_out: float32 [40, 64, 256], P(None, 'space')
- substrates_out: float32 [12, 64, 256], P(None, 'space')
- monomers_out: float32 [14, 64, 256], P(None, 'space')
Inputs may be any that keep to these rules, and one draw needn't show every extreme that they name: Offsets lie in -2 to 2 in both entries and are never both zero; among the row offsets, -2 and 2 each appear twice.
All inputs are finite; a program needn't handle non-finite values. No bound on the sum of `enz_traits` or of `mono_traits` on one device may be relied on, other than what follows from the above.
Results may differ from a plain program's by a relative error of at most 0.00011.
Values sent between devices are 32-bit elements; how exact they have to be, the bound alone decides.
No kernel may reach another device: no remote copies, remote signals or barrier semaphores. Data moves between devices by JAX's collectives and lax.ppermute only.
A program may use at most 128 MiB of HBM per device.

v0:
```python
import jax
import jax.numpy as jnp
from jax import lax
from jax.sharding import PartitionSpec as P

KOFF = 8
DAYS = 2
HIGH = lax.Precision.HIGHEST
YIELD = 0.6


def extended(block, sides, width):
    for axis, dim in sides:
        count = lax.axis_size(axis)
        forward = [(i, i + 1) for i in range(count - 1)]
        forward.append((count - 1, 0))
        backward = [(target, source) for source, target in forward]
        low = lax.ppermute(
            lax.slice_in_dim(block, block.shape[dim] - width, None, axis=dim), axis, forward
        )
        high = lax.ppermute(lax.slice_in_dim(block, 0, width, axis=dim), axis, backward)
        block = jnp.concatenate([low, block, high], axis=dim)
    return block


def cell_update(sums, enz, sub, mono, enz_loss, vmax, kmich, khalf, enz_target):
    n_enz = enz.shape[0]
    made = sums[:n_enz]
    demand = sums[n_enz:]
    pool = enz * (1.0 - enz_loss)[:, None, None] + made
    pick = (enz_target[:, None] == lax.iota(jnp.int32, sub.shape[0])[None, :]).astype(jnp.float32)
    target_sub = jnp.einsum("es,srw->erw", pick, sub, precision=HIGH)
    speed = vmax[:, None, None] * pool / (kmich[:, None, None] + target_sub)
    rate = jnp.einsum("es,erw->srw", pick, speed, precision=HIGH)
    left = sub * jnp.exp(-rate)
    freed = sub - left
    extra = jnp.zeros((mono.shape[0] - sub.shape[0],) + sub.shape[1:], jnp.float32)
    mono_one = mono + jnp.concatenate([freed, extra], 0)
    share = mono_one / (khalf[:, None, None] + demand + mono_one)
    mono_two = mono_one - demand * share
    return (pool, left, mono_two, share)


def pool_update(bio, enz, sub, mono, prod_w, upt_w, enz_loss, vmax, kmich, khalf, enz_target):
    count, rows, width = bio.shape
    flat = bio.reshape(count, rows * width)
    made = jnp.dot(prod_w.T, flat, precision=HIGH, preferred_element_type=jnp.float32)
    need = jnp.dot(upt_w.T, flat, precision=HIGH, preferred_element_type=jnp.float32)
    local = jnp.concatenate([made, need], 0).reshape(-1, rows, width)
    sums = lax.psum(local, "taxa")
    return cell_update(sums, enz, sub, mono, enz_loss, vmax, kmich, khalf, enz_target)


def grow(bio, share, mono_w, uptake_rate, keep):
    gain = jnp.einsum("tm,mrw->trw", mono_w, share, precision=HIGH)
    return bio * (keep[:, None, None] + YIELD * uptake_rate[:, None, None] * gain)


def spread(grown_pad, disperse, offsets, rows):
    fraction = disperse[:, None, None]
    moved_pad = grown_pad * fraction
    centre = grown_pad[:, 2 : 2 + rows]
    total = jnp.zeros_like(centre)
    for k in range(KOFF):
        piece = lax.dynamic_slice_in_dim(moved_pad, 2 - offsets[k, 0], rows, 1)
        total = total + jnp.roll(piece, offsets[k, 1], axis=2)
    return centre - centre * fraction + total / KOFF


def body(
    biomass,
    enzymes,
    substrates,
    monomers,
    enz_traits,
    mono_traits,
    enz_target,
    prod_rate,
    uptake_rate,
    mortality,
    disperse,
    enz_loss,
    vmax,
    kmich,
    khalf,
    offsets,
):
    prod_w = enz_traits.astype(jnp.float32) * prod_rate[:, None]
    mono_w = mono_traits.astype(jnp.float32)
    upt_w = mono_w * uptake_rate[:, None]
    keep = 1.0 - mortality - prod_rate * jnp.sum(enz_traits.astype(jnp.float32), axis=1)
    rows = biomass.shape[1]
    bio = biomass
    for day in range(DAYS):
        enzymes, substrates, monomers, share = pool_update(
            bio,
            enzymes,
            substrates,
            monomers,
            prod_w,
            upt_w,
            enz_loss,
            vmax,
            kmich,
            khalf,
            enz_target,
        )
        grown = grow(bio, share, mono_w, uptake_rate, keep)
        padded = extended(grown, (("space", 1),), 2)
        bio = spread(padded, disperse, offsets, rows)
    return (bio, enzymes, substrates, monomers)


def solution(mesh):
    placed = (
        P("taxa", "space", None),
        P(None, "space", None),
        P(None, "space", None),
        P(None, "space", None),
        P("taxa", None),
        P("taxa", None),
        P(),
        P("taxa"),
        P("taxa"),
        P("taxa"),
        P("taxa"),
        P(),
        P(),
        P(),
        P(),
        P(),
    )
    return jax.shard_map(
        body,
        mesh=mesh,
        in_specs=placed,
        out_specs=(
            P("taxa", "space", None),
            P(None, "space", None),
            P(None, "space", None),
            P(None, "space", None),
        ),
        check_vma=False,
    )
```

profile of v0, /device:TPU:0, one launch (start us, length us, event | category | flops | bytes accessed | tf_op | source)
XLA Modules:
  0.0 286.9 jit_solution(10821046505881652321)
XLA Ops:
  7.2 0.0 all-reduce.5.cloned.1.call-start
  7.2 4.2 %copy.41 = f32[64,8,8,256]{3,1,2,0:T(8,128)S(1)} copy(f32[64,8,8,256]{3,2,1,0:T(8,128)} %bitcast.63) | data formatting | bytes 8388608
  11.4 0.0 copy-start.4
  11.4 0.0 copy-start.14
  11.4 0.0 copy-done.6
  11.4 0.0 copy-done.13
  11.4 2.1 fusion.50
  13.5 2.5 fusion.42
  16.1 0.1 copy.42
  16.3 0.9 copy.31
  17.2 0.0 all-reduce.5.cloned.1.call-update
  17.2 0.0 all-reduce.7.cloned.1.call-start
  17.3 0.0 copy-start.17
  17.3 0.0 copy-start.18
  17.3 0.0 copy-start.8
  17.3 0.0 copy-start.10
  17.3 0.0 copy-start.16
  17.4 0.0 copy-start.19
  17.4 0.0 copy-start.20
  17.4 0.0 copy-start.5
  17.4 0.0 copy-start.15
  17.4 5.4 %copy.35 = f32[512,8,256]{0,2,1:T(8,128)} copy(f32[512,8,256]{2,1,0:T(8,128)} %param.18) | data formatting | bytes 8388608 | tf_op args[0]
  22.8 30.3 %all-reduce.5.cloned.1.call-done = f32[54,8,256]{2,0,1:T(8,128)} async-done(((f32[54,8,256]{2,0,1:T(8,128)}), f32[54,8,256]{2,0,1:T(8,128)}) %all-reduce.5.cloned.1.call-update) | async-done | bytes 442384 | tf_op jit(solution)/shard_map/psum | solution.py:50
  53.1 1.4 fusion.35
  54.5 0.9 copy_subtract_fusion
  55.4 7.1 %bitcast_multiply_fusion.1 = f32[512,8,256]{0,2,1:T(8,128)S(1)} fusion(f32[512,8,256]{0,2,1:T(8,128)} %copy.35, f32[512]{0:T(512)S(1)} %get-tuple-element.56, f32[512]{0:T(512)S(1)} %get-tuple-element.55, s32[512,14]{0,1:T(8,128)S(1)} %copy-done.6, f32[54,8,256]{2,0,1:T(8,128)} %all-reduce.5.cloned.1.call-done, f32[14]{0:T(128)S(1)} %copy-done.15, ...), kind=kOutput, calls=%fused_computation.71 | convolution fusion | flops 179428352 | bytes 8765496 | tf_op jit(solution)/shard_map/tm,mrw->trw/dot_general | solution.py:55
  62.5 0.0 copy-start.1
  62.5 2.0 copy-done.1
  64.5 0.2 fusion.63
  64.7 1.5 collective-permute-start
  66.2 3.2 %collective-permute-start.1 = (f32[512,2,256]{0,2,1:T(8,128)S(1)}, f32[512,2,256]{0,2,1:T(8,128)}, u32[]{:S(2)}, u32[]{:S(2)}) collective-permute-start(f32[512,2,256]{0,2,1:T(8,128)S(1)} %get-tuple-element.34), channel_id=1, source_target_pairs={{4,0},{8,4},{12,8},{16,12},{20,16},{24,20},{28,24},{0,28},{5,1},{9... | collective-permute-start | bytes 3145736 | tf_op jit(solution)/shard_map/ppermute | solution.py:21
  69.5 0.7 fusion.64
  95.8 14.2 %collective-permute-done = f32[512,2,256]{0,2,1:T(8,128)S(1)} collective-permute-done((f32[512,2,256]{0,2,1:T(8,128)S(1)}, f32[512,2,256]{0,2,1:T(8,128)S(1)}, u32[]{:S(2)}, u32[]{:S(2)}) %collective-permute-start) | collective-permute-done | bytes 1048608 | tf_op jit(solution)/shard_map/ppermute | solution.py:18
  110.0 2.3 collective-permute-done.1
  112.3 3.0 %maximum_multiply_fusion = f32[512,12,256]{0,2,1:T(8,128)S(1)} fusion(f32[512,2,256]{0,2,1:T(8,128)} %collective-permute-done.1, f32[512,8,256]{0,2,1:T(8,128)} %copy-done.1, f32[512,2,256]{0,2,1:T(8,128)S(1)} %collective-permute-done, f32[512]{0:T(512)S(1)} %copy-done.12), kind=kLoop, calls=%fused_computation.32 | loop fusion | flops 4718592 | bytes 12584960 | tf_op jit(solution)/shard_map/mul | solution.py:61
  115.3 12.3 %constant_dynamic-slice_fusion.15 = (f32[512,8,256]{0,2,1:T(8,128)}, f32[512,8,256]{0,2,1:T(8,128)}, f32[512,8,256]{0,2,1:T(8,128)}, f32[512,8,256]{0,2,1:T(8,12...) fusion(f32[512,12,256]{0,2,1:T(8,128)S(1)} %maximum_multiply_fusion, ...), kind=kLoop, calls=%fused_computation.124 | loop fusion | bytes 67108896 | tf_op jit(solution)/shard_map/dynamic_slice | solution.py:65
  127.6 16.5 %fusion = f32[512,8,256]{0,2,1:T(8,128)S(1)} fusion(f32[512,8,256]{0,2,1:T(8,128)} %copy-done.1, s32[]{:T(128)S(6)} %select_n.95, f32[512,8,256]{0,2,1:T(8,128)} %get-tuple-element.24, s32[]{:T(128)S(6)} %select_n.93, f32[512,8,256]{0,2,1:T(8,128)} %get-tuple-element.25, s32[]{:T(128)S(6)} %select_n.91, f32[512,8,256]{0,2,1:T(8,128)} %get-tuple-element.26, ...), kind=kLoop, calls=%fused_computation.36 | loop fusion | flops 19922944 | bytes 41945120 | tf_op jit(solution)/shard_map/add | solution.py:67
  144.1 0.0 copy-start
  144.1 3.5 %fusion.49 = f32[14,2048]{1,0:T(8,128)S(1)} fusion(f32[512,2048]{0,1:T(8,128)S(1)} %bitcast.59, s32[512,14]{0,1:T(8,128)S(1)} %copy-done.6, f32[512]{0:T(512)S(1)} %copy-done.13), kind=kOutput, calls=%fused_computation.105 | convolution fusion | flops 176175104 | bytes 4339712 | tf_op jit(solution)/shard_map/dot_general | solution.py:48
  147.7 0.0 copy-start.9
  147.7 0.0 copy-start.7
  147.7 4.0 %fusion.41 = f32[40,2048]{1,0:T(8,128)S(1)} fusion(f32[512,2048]{0,1:T(8,128)S(1)} %bitcast.60, s32[512,40]{0,1:T(8,128)S(1)} %copy-done.4, f32[512]{0:T(512)S(1)} %copy-done.14), kind=kOutput, calls=%fused_computation.96 | convolution fusion | flops 503357440 | bytes 4605952 | tf_op jit(solution)/shard_map/dot_general | solution.py:47
  151.8 0.1 copy.43
  151.9 0.9 copy.36
  152.9 0.0 all-reduce.7.cloned.1.call-update
  152.9 32.7 %all-reduce.7.cloned.1.call-done = f32[54,8,256]{2,0,1:T(8,128)} async-done(((f32[54,8,256]{2,0,1:T(8,128)}), f32[54,8,256]{2,0,1:T(8,128)}) %all-reduce.7.cloned.1.call-update) | async-done | bytes 442384 | tf_op jit(solution)/shard_map/psum | solution.py:50
  185.6 1.1 slice_add_fusion
  186.7 0.4 fusion.34
  187.1 0.2 fusion.65
  187.3 1.0 multiply_subtract_fusion.2
  188.4 7.2 %bitcast_multiply_fusion = f32[512,8,256]{0,2,1:T(8,128)S(1)} fusion(f32[512,8,256]{0,2,1:T(8,128)} %copy-done, f32[512]{0:T(512)S(1)} %get-tuple-element.56, f32[512]{0:T(512)S(1)} %get-tuple-element.55, s32[512,14]{0,1:T(8,128)S(1)} %copy-done.6, f32[14,8,256]{2,0,1:T(8,128)S(1)} %get-tuple-element.14, f32[54,8,256]{2,0,1:T(8,128)} %all-reduce.7.cloned.1.call-done, ...), kind=kOutput, calls=%fused_computation.70 | convolution fusion | flops 179399680 | bytes 8667192 | tf_op jit(solution)/shard_map/tm,mrw->trw/dot_general | solution.py:55
  195.5 0.0 copy-start.2
  195.6 0.2 fusion.62
  195.8 1.5 collective-permute-start.2
  197.3 3.3 %collective-permute-start.3 = (f32[512,2,256]{0,2,1:T(8,128)S(1)}, f32[512,2,256]{0,2,1:T(8,128)S(1)}, u32[]{:S(2)}, u32[]{:S(2)}) collective-permute-start(f32[512,2,256]{0,2,1:T(8,128)S(1)} %get-tuple-element.32), channel_id=1, source_target_pairs={{4,0},{8,4},{12,8},{16,12},{20,16},{24,20},{28,24},{0,28},{5,1},{9... | collective-permute-start | bytes 3145736 | tf_op jit(solution)/shard_map/ppermute | solution.py:21
  200.6 0.8 copy.38
  201.4 0.7 copy.40
  202.1 0.7 copy.39
  202.8 38.3 %collective-permute-done.2 = f32[512,2,256]{0,2,1:T(8,128)S(1)} collective-permute-done((f32[512,2,256]{0,2,1:T(8,128)S(1)}, f32[512,2,256]{0,2,1:T(8,128)S(1)}, u32[]{:S(2)}, u32[]{:S(2)}) %collective-permute-start.2) | collective-permute-done | bytes 1048608 | tf_op jit(solution)/shard_map/ppermute | solution.py:18
  241.1 2.2 collective-permute-done.3
  243.3 0.8 maximum_multiply_fusion.1
  244.1 12.3 %constant_dynamic-slice_fusion.7 = (f32[512,8,256]{0,2,1:T(8,128)}, f32[512,8,256]{0,2,1:T(8,128)}, f32[512,8,256]{0,2,1:T(8,128)}, f32[512,8,256]{0,2,1:T(8,128...) fusion(f32[512,12,256]{0,2,1:T(8,128)S(1)} %maximum_multiply_fusion.1,, ...), kind=kLoop, calls=%fused_computation.116 | loop fusion | bytes 67108896 | tf_op jit(solution)/shard_map/dynamic_slice | solution.py:65
  256.4 18.2 %fusion.1 = f32[512,8,256]{0,2,1:T(8,128)} fusion(f32[512,8,256]{0,2,1:T(8,128)} %copy-done.2, s32[]{:T(128)S(6)} %select_n.95, f32[512,8,256]{0,2,1:T(8,128)} %get-tuple-element.16, s32[]{:T(128)S(6)} %select_n.93, f32[512,8,256]{0,2,1:T(8,128)} %get-tuple-element.17, s32[]{:T(128)S(6)} %select_n.91, f32[512,8,256]{0,2,1:T(8,128)} %get-tuple-element.18, ...), kind=kLoop, calls=%fused_computation.37 | loop fusion | flops 19922944 | bytes 41945120 | tf_op jit(solution)/shard_map/add | solution.py:67
  274.6 5.4 %copy.37 = f32[512,8,256]{2,1,0:T(8,128)} copy(f32[512,8,256]{0,2,1:T(8,128)} %fusion.1) | data formatting | bytes 8388608
  (30 shorter events, 0.2 us)
Async XLA Ops:
  7.2 46.0 %all-reduce.5.cloned.1.call-start = ((), (), s32[]{:S(2)}) async-start(), calls=%async_computation | async-start | bytes 917504 | tf_op jit(solution)/shard_map/psum | solution.py:50
  7.2 4.2 %copy-start.6 = (s32[512,14]{0,1:T(8,128)S(1)}, s32[512,14]{0,1:T(8,128)}, u32[]{:S(2)}) copy-start(s32[512,14]{0,1:T(8,128)} %param.23) | copy-start | bytes 86020
  7.2 4.2 %copy-start.13 = (f32[512]{0:T(512)S(1)}, f32[512]{0:T(512)}, u32[]{:S(2)}) copy-start(f32[512]{0:T(512)} %param.26) | copy-start | bytes 6148
  11.4 2.1 copy-start.4
  11.4 2.1 copy-start.14
  17.2 168.3 %all-reduce.7.cloned.1.call-start = ((), (), s32[]{:S(2)}) async-start(), calls=%async_computation.1 | async-start | bytes 917504 | tf_op jit(solution)/shard_map/psum | solution.py:50
  17.3 5.5 %copy-start.17 = (f32[512]{0:T(512)S(1)}, f32[512]{0:T(512)}, u32[]{:S(2)}) copy-start(f32[512]{0:T(512)} %param.27) | copy-start | bytes 6148
  17.3 5.5 %copy-start.18 = (f32[40]{0:T(128)S(1)}, f32[40]{0:T(128)}, u32[]{:S(2)}) copy-start(f32[40]{0:T(128)} %param.29) | copy-start | bytes 484
  17.3 35.8 %copy-start.8 = (f32[40,8,256]{2,1,0:T(8,128)S(1)}, f32[40,8,256]{2,1,0:T(8,128)}, u32[]{:S(2)}) copy-start(f32[40,8,256]{2,1,0:T(8,128)} %param.19) | copy-start | bytes 983044
  17.3 35.8 %copy-start.10 = (f32[12,8,256]{2,1,0:T(8,128)S(1)}, f32[12,8,256]{2,1,0:T(8,128)}, u32[]{:S(2)}) copy-start(f32[12,8,256]{2,1,0:T(8,128)} %param.20) | copy-start | bytes 294916
  17.3 35.8 %copy-start.16 = (s32[40]{0:T(128)S(1)}, s32[40]{0:T(128)}, u32[]{:S(2)}) copy-start(s32[40]{0:T(128)} %param.24) | copy-start | bytes 484
  17.4 35.8 %copy-start.19 = (f32[40]{0:T(128)S(1)}, f32[40]{0:T(128)}, u32[]{:S(2)}) copy-start(f32[40]{0:T(128)} %param.31) | copy-start | bytes 484
  17.4 35.8 %copy-start.20 = (f32[40]{0:T(128)S(1)}, f32[40]{0:T(128)}, u32[]{:S(2)}) copy-start(f32[40]{0:T(128)} %param.30) | copy-start | bytes 484
  17.4 38.0 %copy-start.5 = (f32[14,8,256]{2,1,0:T(8,128)S(1)}, f32[14,8,256]{2,1,0:T(8,128)}, u32[]{:S(2)}) copy-start(f32[14,8,256]{2,1,0:T(8,128)} %param.21) | copy-start | bytes 344068
  17.4 38.0 %copy-start.15 = (f32[14]{0:T(128)S(1)}, f32[14]{0:T(128)}, u32[]{:S(2)}) copy-start(f32[14]{0:T(128)} %param.32) | copy-start | bytes 172
  62.5 2.0 copy-start.1
  64.5 5.0 %copy-start.11 = (s32[8,2]{0,1:T(2,128)S(1)}, s32[8,2]{0,1:T(2,128)}, u32[]{:S(2)}) copy-start(s32[8,2]{0,1:T(2,128)} %param.33) | copy-start | bytes 196
  64.5 47.8 %copy-start.12 = (f32[512]{0:T(512)S(1)}, f32[512]{0:T(512)}, u32[]{:S(2)}) copy-start(f32[512]{0:T(512)} %param.28) | copy-start | bytes 6148
  64.7 45.3 %collective-permute-start = (f32[512,2,256]{0,2,1:T(8,128)S(1)}, f32[512,2,256]{0,2,1:T(8,128)S(1)}, u32[]{:S(2)}, u32[]{:S(2)}) collective-permute-start(f32[512,2,256]{0,2,1:T(8,128)S(1)} %get-tuple-element.33), channel_id=1, source_target_pairs={{0,4},{4,8},{8,12},{12,16},{16,20},{20,24},{24,28},{28,0},{1,5},{5... | collective-permute-start | bytes 3145736 | tf_op jit(solution)/shard_map/ppermute | solution.py:18
  66.2 46.1 %collective-permute-start.1 = (f32[512,2,256]{0,2,1:T(8,128)S(1)}, f32[512,2,256]{0,2,1:T(8,128)}, u32[]{:S(2)}, u32[]{:S(2)}) collective-permute-start(f32[512,2,256]{0,2,1:T(8,128)S(1)} %get-tuple-element.34), channel_id=1, source_target_pairs={{4,0},{8,4},{12,8},{16,12},{20,16},{24,20},{28,24},{0,28},{5,1},{9... | collective-permute-start | bytes 3145736 | tf_op jit(solution)/shard_map/ppermute | solution.py:21
  144.1 7.6 %copy-start = (f32[512,8,256]{0,2,1:T(8,128)}, f32[512,8,256]{0,2,1:T(8,128)S(1)}, u32[]{:S(2)}) copy-start(f32[512,8,256]{0,2,1:T(8,128)S(1)} %fusion) | copy-start | bytes 12582916
  147.7 37.9 %copy-start.3 = (f32[54,8,256]{2,0,1:T(8,128)S(1)}, f32[54,8,256]{2,0,1:T(8,128)}, u32[]{:S(2)}) copy-start(f32[54,8,256]{2,0,1:T(8,128)} %all-reduce.5.cloned.1.call-done) | copy-start | bytes 1327108
  147.7 37.9 %copy-start.9 = (f32[40,8,256]{2,1,0:T(8,128)S(1)}, f32[40,8,256]{2,1,0:T(8,128)}, u32[]{:S(2)}) copy-start(f32[40,8,256]{2,1,0:T(8,128)} %param.19) | copy-start | bytes 983044
  147.7 39.0 %copy-start.7 = (f32[12,8,256]{2,0,1:T(8,128)S(1)}, f32[12,8,256]{2,0,1:T(8,128)}, u32[]{:S(2)}) copy-start(f32[12,8,256]{2,0,1:T(8,128)} %get-tuple-element.52) | copy-start | bytes 294916
  195.5 47.7 %copy-start.2 = (f32[512,8,256]{0,2,1:T(8,128)}, f32[512,8,256]{0,2,1:T(8,128)S(1)}, u32[]{:S(2)}) copy-start(f32[512,8,256]{0,2,1:T(8,128)S(1)} %bitcast_multiply_fusion) | copy-start | bytes 12582916
  195.8 45.3 %collective-permute-start.2 = (f32[512,2,256]{0,2,1:T(8,128)S(1)}, f32[512,2,256]{0,2,1:T(8,128)S(1)}, u32[]{:S(2)}, u32[]{:S(2)}) collective-permute-start(f32[512,2,256]{0,2,1:T(8,128)S(1)} %get-tuple-element.31), channel_id=1, source_target_pairs={{0,4},{4,8},{8,12},{12,16},{16,20},{20,24},{24,28},{28,0},{1,5},{5... | collective-permute-start | bytes 3145736 | tf_op jit(solution)/shard_map/ppermute | solution.py:18
  197.3 46.0 %collective-permute-start.3 = (f32[512,2,256]{0,2,1:T(8,128)S(1)}, f32[512,2,256]{0,2,1:T(8,128)S(1)}, u32[]{:S(2)}, u32[]{:S(2)}) collective-permute-start(f32[512,2,256]{0,2,1:T(8,128)S(1)} %get-tuple-element.32), channel_id=1, source_target_pairs={{4,0},{8,4},{12,8},{16,12},{20,16},{24,20},{28,24},{0,28},{5,1},{9... | collective-permute-start | bytes 3145736 | tf_op jit(solution)/shard_map/ppermute | solution.py:21
Sparse Core Ops, SparseCore 0:
  17.3 35.7 all-reduce.4
  153.0 32.5 all-reduce.6
where the time goes:
time: 288 us; the launch traced here: 287 us
  waiting for transfers between devices  120 us (42%)
  local copies, waits for them, and re-layouts  47.1 us (16%)
  other arithmetic  40.9 us (14%)
  between operations  40 us (14%)
  matrix products  29.2 us (10%)
  starting transfers between devices  9.63 us (3%)
    psum x2, waiting for transfers between devices, pool_update(): sums = lax.psum(local, 'taxa')  63 us
    ppermute x2, waiting for transfers between devices, extended(): lax.ppermute(lax.slice_in_dim(block, block.shape[dim] - width, None, axis...  52.5 us
    add x2, other arithmetic, spread(): return centre - centre * fraction + total / KOFF  34.7 us
    dynamic_slice x2, local copies, waits for them, and re-layouts, spread(): piece = lax.dynamic_slice_in_dim(moved_pad, 2 - offsets[k, 0], rows, 1)  24.5 us
    unnamed x50, local copies, waits for them, and re-layouts  19.6 us
    dot_general x2, matrix products, grow(): gain = jnp.einsum('tm,mrw->trw', mono_w, share, precision=HIGH)  14.2 us
    dot_general x2, matrix products, pool_update(): jnp.dot(prod_w.T, flat, precision=HIGH, preferred_element_type=jnp.float32)  6.51 us
    ppermute x2, starting transfers between devices, extended(): lax.ppermute(lax.slice_in_dim(block, 0, width, axis=dim), axis, backward)  6.5 us
  transfers between devices with their start and end apart: 6, of which 6 were waited for; matrix products, arithmetic and copies ran while one was open for 3% of the time, Pallas kernels for 0%

commit v1 on v0

--- a/solution.py
+++ b/solution.py
@@ -47,7 +47,7 @@
     made = jnp.dot(prod_w.T, flat, precision=HIGH, preferred_element_type=jnp.float32)
     need = jnp.dot(upt_w.T, flat, precision=HIGH, preferred_element_type=jnp.float32)
     local = jnp.concatenate([made, need], 0).reshape(-1, rows, width)
-    sums = lax.psum(local, "taxa")
+    sums = jnp.sum(lax.all_gather(local, "taxa"), axis=0)
     return cell_update(sums, enz, sub, mono, enz_loss, vmax, kmich, khalf, enz_target)
 
 

time: 288 us -> 264 us (0.917)
  waiting for transfers between devices: 120 us -> 98.4 us
  matrix products: 29.2 us -> 24.9 us
    psum x2 -> x0, waiting for transfers between devices: 63 us -> none  [pool_update(): sums = lax.psum(local, 'taxa')]
    all_gather x0 -> x2, waiting for transfers between devices: none -> 37.3 us  [pool_update(): sums = jnp.sum(lax.all_gather(local, 'taxa'), axis=0)]
    ppermute x2, waiting for transfers between devices: 52.5 us -> 56.9 us  [extended(): lax.ppermute(lax.slice_in_dim(block, block.shape[dim] - width, None, axis...]
    reduce_sum x0 -> x2, other arithmetic: none -> 3.28 us  [pool_update(): sums = jnp.sum(lax.all_gather(local, 'taxa'), axis=0)]
    unnamed x50 -> x43, local copies, waits for them, and re-layouts: 19.6 us -> 18.7 us
where the time goes in v1:
time: 264 us; the launch traced here: 263 us
  waiting for transfers between devices  98.4 us (37%)
  local copies, waits for them, and re-layouts  47 us (18%)
  other arithmetic  43.5 us (16%)
  between operations  39.8 us (15%)
  matrix products  24.9 us (9%)
  starting transfers between devices  9.58 us (4%)
    ppermute x2, waiting for transfers between devices, extended(): lax.ppermute(lax.slice_in_dim(block, block.shape[dim] - width, None, axis...  56.9 us
    all_gather x2, waiting for transfers between devices, pool_update(): sums = jnp.sum(lax.all_gather(local, 'taxa'), axis=0)  37.3 us
    add x2, other arithmetic, spread(): return centre - centre * fraction + total / KOFF  34.8 us
    dynamic_slice x2, local copies, waits for them, and re-layouts, spread(): piece = lax.dynamic_slice_in_dim(moved_pad, 2 - offsets[k, 0], rows, 1)  24.5 us
    unnamed x43, local copies, waits for them, and re-layouts  18.7 us
    dot_general x2, matrix products, grow(): gain = jnp.einsum('tm,mrw->trw', mono_w, share, precision=HIGH)  11.4 us
    dot_general x2, matrix products, pool_update(): jnp.dot(prod_w.T, flat, precision=HIGH, preferred_element_type=jnp.float32)  6.5 us
    ppermute x2, starting transfers between devices, extended(): lax.ppermute(lax.slice_in_dim(block, 0, width, axis=dim), axis, backward)  6.5 us
  transfers between devices with their start and end apart: 6, of which 6 were waited for; matrix products, arithmetic and copies ran while one was open for 3% of the time, Pallas kernels for 0%

profile of v1, /device:TPU:0, one launch (start us, length us, event | category | flops | bytes accessed | tf_op | source)
XLA Modules:
  0.0 263.2 jit_solution(14949510732037046983)
XLA Ops:
  7.2 0.0 all-gather.3.cloned.1.call-start
  7.2 0.0 copy-start.4
  7.2 0.0 copy-start.10
  7.2 4.2 %copy.44 = f32[64,8,8,256]{3,1,2,0:T(8,128)S(1)} copy(f32[64,8,8,256]{3,2,1,0:T(8,128)} %bitcast.65) | data formatting | bytes 8388608
  11.4 0.0 copy-start.7
  11.4 0.0 copy-start.11
  11.5 2.5 fusion.48
  14.0 2.1 fusion.56
  16.1 0.1 copy.45
  16.3 0.8 slice_bitcast_fusion.1
  17.1 0.0 all-gather.3.cloned.1.call-update
  17.1 0.0 copy-start.17
  17.1 0.0 copy-start.14
  17.1 0.0 copy-start.5
  17.1 0.0 copy-start.12
  17.1 0.0 copy-start.3
  17.2 0.0 copy-start.15
  17.2 0.0 copy-start.16
  17.2 0.0 all-gather.5.cloned.1.call-start
  17.2 5.3 %copy.34 = f32[512,8,256]{0,2,1:T(8,128)} copy(f32[512,8,256]{2,1,0:T(8,128)} %param.18) | data formatting | bytes 8388608 | tf_op args[0]
  22.6 0.3 fusion.42
  23.0 17.7 %all-gather.3.cloned.1.call-done = f32[4,54,8,256]{3,2,1,0:T(8,128)} async-done(((f32[1,54,8,256]{3,2,1,0:T(8,128)}), f32[4,54,8,256]{3,2,1,0:T(8,128)}) %all-gather.3.cloned.1.call-update) | async-done | bytes 1769488 | tf_op jit(solution)/shard_map/all_gather | solution.py:50
  40.7 1.6 reduce_sum.28
  42.4 0.2 fusion.39
  42.6 0.3 copy_subtract_fusion
  43.0 0.0 copy-done.6
  43.0 0.0 copy-done.13
  43.0 5.7 %bitcast_multiply_fusion.1 = f32[512,8,256]{0,2,1:T(8,128)S(1)} fusion(f32[512,8,256]{0,2,1:T(8,128)} %copy.34, f32[512]{0:T(512)S(1)} %get-tuple-element.58, f32[512]{0:T(512)S(1)} %get-tuple-element.57, f32[14,8,256]{2,1,0:T(8,128)S(1)} %slice.113, f32[14]{0:T(128)S(1)} %copy-done.13, f32[14,8,256]{2,1,0:T(8,128)S(1)} %copy-done.6, ...), kind=kOutput, calls=%fused_computation.71 | convolution fusion | flops 179428352 | bytes 8749112 | tf_op jit(solution)/shard_map/tm,mrw->trw/dot_general | solution.py:55
  48.7 0.0 copy-start.1
  48.7 2.0 copy-done.1
  50.7 1.2 fusion.72
  51.9 1.5 collective-permute-start
  53.3 3.2 %collective-permute-start.1 = (f32[512,2,256]{0,2,1:T(8,128)S(1)}, f32[512,2,256]{0,2,1:T(8,128)}, u32[]{:S(2)}, u32[]{:S(2)}) collective-permute-start(f32[512,2,256]{0,2,1:T(8,128)S(1)} %get-tuple-element.36), channel_id=1, source_target_pairs={{4,0},{8,4},{12,8},{16,12},{20,16},{24,20},{28,24},{0,28},{5,1},{9... | collective-permute-start | bytes 3145736 | tf_op jit(solution)/shard_map/ppermute | solution.py:21
  56.6 0.7 fusion.73
  82.7 16.2 %collective-permute-done = f32[512,2,256]{0,2,1:T(8,128)} collective-permute-done((f32[512,2,256]{0,2,1:T(8,128)}, f32[512,2,256]{0,2,1:T(8,128)}, u32[]{:S(2)}, u32[]{:S(2)}) %collective-permute-start) | collective-permute-done | bytes 1048608 | tf_op jit(solution)/shard_map/ppermute | solution.py:18
  98.9 2.0 collective-permute-done.1
  100.9 3.2 %maximum_multiply_fusion = f32[512,12,256]{0,2,1:T(8,128)S(1)} fusion(f32[512,2,256]{0,2,1:T(8,128)} %collective-permute-done.1, f32[512,8,256]{0,2,1:T(8,128)} %copy-done.1, f32[512,2,256]{0,2,1:T(8,128)} %collective-permute-done, f32[512]{0:T(512)S(1)} %copy-done.9), kind=kLoop, calls=%fused_computation.32 | loop fusion | flops 4718592 | bytes 12584960 | tf_op jit(solution)/shard_map/mul | solution.py:61
  104.1 12.3 %constant_dynamic-slice_fusion.15 = (f32[512,8,256]{0,2,1:T(8,128)}, f32[512,8,256]{0,2,1:T(8,128)}, f32[512,8,256]{0,2,1:T(8,128)}, f32[512,8,256]{0,2,1:T(8,12...) fusion(f32[512,12,256]{0,2,1:T(8,128)S(1)} %maximum_multiply_fusion, ...), kind=kLoop, calls=%fused_computation.133 | loop fusion | bytes 67108896 | tf_op jit(solution)/shard_map/dynamic_slice | solution.py:65
  116.4 16.5 %fusion = f32[512,8,256]{0,2,1:T(8,128)S(1)} fusion(f32[512,8,256]{0,2,1:T(8,128)} %copy-done.1, s32[]{:T(128)S(6)} %select_n.95, f32[512,8,256]{0,2,1:T(8,128)} %get-tuple-element.26, s32[]{:T(128)S(6)} %select_n.93, f32[512,8,256]{0,2,1:T(8,128)} %get-tuple-element.27, s32[]{:T(128)S(6)} %select_n.91, f32[512,8,256]{0,2,1:T(8,128)} %get-tuple-element.28, ...), kind=kLoop, calls=%fused_computation.36 | loop fusion | flops 19922944 | bytes 41945120 | tf_op jit(solution)/shard_map/add | solution.py:67
  132.9 0.0 copy-start
  132.9 4.0 %fusion.47 = f32[40,2048]{1,0:T(8,128)S(1)} fusion(f32[512,2048]{0,1:T(8,128)S(1)} %bitcast.61, s32[512,40]{0,1:T(8,128)S(1)} %copy-done.4, f32[512]{0:T(512)S(1)} %copy-done.10), kind=kOutput, calls=%fused_computation.105 | convolution fusion | flops 503357440 | bytes 4605952 | tf_op jit(solution)/shard_map/dot_general | solution.py:47
  136.9 3.5 %fusion.55 = f32[14,2048]{1,0:T(8,128)S(1)} fusion(f32[512,2048]{0,1:T(8,128)S(1)} %bitcast.62, s32[512,14]{0,1:T(8,128)S(1)} %copy-done.7, f32[512]{0:T(512)S(1)} %copy-done.11), kind=kOutput, calls=%fused_computation.114 | convolution fusion | flops 176175104 | bytes 4339712 | tf_op jit(solution)/shard_map/dot_general | solution.py:48
  140.5 0.1 copy.46
  140.7 0.8 slice_bitcast_fusion
  141.5 0.0 all-gather.5.cloned.1.call-update
  141.5 0.3 fusion.61
  141.8 19.6 %all-gather.5.cloned.1.call-done = f32[4,54,8,256]{3,2,1,0:T(8,128)} async-done(((f32[1,54,8,256]{3,2,1,0:T(8,128)}), f32[4,54,8,256]{3,2,1,0:T(8,128)}) %all-gather.5.cloned.1.call-update) | async-done | bytes 1769488 | tf_op jit(solution)/shard_map/all_gather | solution.py:50
  161.4 1.6 reduce_sum.29
  163.1 0.9 fusion.38
  164.0 0.3 fusion.74
  164.4 0.2 fusion.46
  164.5 5.7 %bitcast_multiply_fusion = f32[512,8,256]{0,2,1:T(8,128)S(1)} fusion(f32[512,8,256]{0,2,1:T(8,128)} %copy-done, f32[512]{0:T(512)S(1)} %get-tuple-element.58, f32[512]{0:T(512)S(1)} %get-tuple-element.57, f32[14,8,256]{2,0,1:T(8,128)S(1)} %get-tuple-element.14, f32[14,8,256]{2,1,0:T(8,128)S(1)} %slice.117, f32[14]{0:T(128)S(1)} %copy-done.13, ...), kind=kOutput, calls=%fused_computation.70 | convolution fusion | flops 179399680 | bytes 8650808 | tf_op jit(solution)/shard_map/tm,mrw->trw/dot_general | solution.py:55
  170.3 0.0 copy-start.2
  170.3 0.2 fusion.71
  170.5 1.5 collective-permute-start.2
  172.0 3.2 %collective-permute-start.3 = (f32[512,2,256]{0,2,1:T(8,128)S(1)}, f32[512,2,256]{0,2,1:T(8,128)S(1)}, u32[]{:S(2)}, u32[]{:S(2)}) collective-permute-start(f32[512,2,256]{0,2,1:T(8,128)S(1)} %get-tuple-element.34), channel_id=1, source_target_pairs={{4,0},{8,4},{12,8},{16,12},{20,16},{24,20},{28,24},{0,28},{5,1},{9... | collective-permute-start | bytes 3145736 | tf_op jit(solution)/shard_map/ppermute | solution.py:21
  175.3 0.7 copy.39
  176.0 0.7 copy.38
  176.7 40.6 %collective-permute-done.2 = f32[512,2,256]{0,2,1:T(8,128)S(1)} collective-permute-done((f32[512,2,256]{0,2,1:T(8,128)S(1)}, f32[512,2,256]{0,2,1:T(8,128)S(1)}, u32[]{:S(2)}, u32[]{:S(2)}) %collective-permute-start.2) | collective-permute-done | bytes 1048608 | tf_op jit(solution)/shard_map/ppermute | solution.py:18
  217.3 2.2 collective-permute-done.3
  219.5 0.8 maximum_multiply_fusion.1
  220.4 12.3 %constant_dynamic-slice_fusion.7 = (f32[512,8,256]{0,2,1:T(8,128)}, f32[512,8,256]{0,2,1:T(8,128)}, f32[512,8,256]{0,2,1:T(8,128)}, f32[512,8,256]{0,2,1:T(8,128...) fusion(f32[512,12,256]{0,2,1:T(8,128)S(1)} %maximum_multiply_fusion.1,, ...), kind=kLoop, calls=%fused_computation.125 | loop fusion | bytes 67108896 | tf_op jit(solution)/shard_map/dynamic_slice | solution.py:65
  232.6 18.2 %fusion.1 = f32[512,8,256]{0,2,1:T(8,128)} fusion(f32[512,8,256]{0,2,1:T(8,128)} %copy-done.2, s32[]{:T(128)S(6)} %select_n.95, f32[512,8,256]{0,2,1:T(8,128)} %get-tuple-element.18, s32[]{:T(128)S(6)} %select_n.93, f32[512,8,256]{0,2,1:T(8,128)} %get-tuple-element.19, s32[]{:T(128)S(6)} %select_n.91, f32[512,8,256]{0,2,1:T(8,128)} %get-tuple-element.20, ...), kind=kLoop, calls=%fused_computation.37 | loop fusion | flops 19922944 | bytes 41945120 | tf_op jit(solution)/shard_map/add | solution.py:67
  250.9 5.4 %copy.37 = f32[512,8,256]{2,1,0:T(8,128)} copy(f32[512,8,256]{0,2,1:T(8,128)} %fusion.1) | data formatting | bytes 8388608
  (26 shorter events, 0.2 us)
Async XLA Ops:
  7.2 33.5 %all-gather.3.cloned.1.call-start = ((), (), s32[]{:S(2)}) async-start(), calls=%async_computation | async-start | bytes 2211840 | tf_op jit(solution)/shard_map/all_gather | solution.py:50
  7.2 4.2 %copy-start.4 = (s32[512,40]{0,1:T(8,128)S(1)}, s32[512,40]{0,1:T(8,128)}, u32[]{:S(2)}) copy-start(s32[512,40]{0,1:T(8,128)} %param.22) | copy-start | bytes 245764
  7.2 4.2 %copy-start.10 = (f32[512]{0:T(512)S(1)}, f32[512]{0:T(512)}, u32[]{:S(2)}) copy-start(f32[512]{0:T(512)} %param.25) | copy-start | bytes 6148
  11.4 2.6 copy-start.7
  11.4 2.6 copy-start.11
  17.1 5.5 %copy-start.17 = (f32[40]{0:T(128)S(1)}, f32[40]{0:T(128)}, u32[]{:S(2)}) copy-start(f32[40]{0:T(128)} %param.29) | copy-start | bytes 484
  17.1 5.5 %copy-start.14 = (f32[512]{0:T(512)S(1)}, f32[512]{0:T(512)}, u32[]{:S(2)}) copy-start(f32[512]{0:T(512)} %param.27) | copy-start | bytes 6148
  17.1 5.5 %copy-start.5 = (f32[12,8,256]{2,1,0:T(8,128)S(1)}, f32[12,8,256]{2,1,0:T(8,128)}, u32[]{:S(2)}) copy-start(f32[12,8,256]{2,1,0:T(8,128)} %param.20) | copy-start | bytes 294916
  17.1 5.5 %copy-start.12 = (s32[40]{0:T(128)S(1)}, s32[40]{0:T(128)}, u32[]{:S(2)}) copy-start(s32[40]{0:T(128)} %param.24) | copy-start | bytes 484
  17.1 25.2 %copy-start.3 = (f32[40,8,256]{2,1,0:T(8,128)S(1)}, f32[40,8,256]{2,1,0:T(8,128)}, u32[]{:S(2)}) copy-start(f32[40,8,256]{2,1,0:T(8,128)} %param.19) | copy-start | bytes 983044
  17.2 25.2 %copy-start.15 = (f32[40]{0:T(128)S(1)}, f32[40]{0:T(128)}, u32[]{:S(2)}) copy-start(f32[40]{0:T(128)} %param.31) | copy-start | bytes 484
  17.2 25.2 %copy-start.16 = (f32[40]{0:T(128)S(1)}, f32[40]{0:T(128)}, u32[]{:S(2)}) copy-start(f32[40]{0:T(128)} %param.30) | copy-start | bytes 484
  17.2 144.3 %all-gather.5.cloned.1.call-start = ((), (), s32[]{:S(2)}) async-start(), calls=%async_computation.1 | async-start | bytes 2211840 | tf_op jit(solution)/shard_map/all_gather | solution.py:50
  22.5 20.4 %copy-start.6 = (f32[14,8,256]{2,1,0:T(8,128)S(1)}, f32[14,8,256]{2,1,0:T(8,128)}, u32[]{:S(2)}) copy-start(f32[14,8,256]{2,1,0:T(8,128)} %param.21) | copy-start | bytes 344068
  22.6 20.4 %copy-start.13 = (f32[14]{0:T(128)S(1)}, f32[14]{0:T(128)}, u32[]{:S(2)}) copy-start(f32[14]{0:T(128)} %param.32) | copy-start | bytes 172
  48.7 2.0 copy-start.1
  50.7 5.9 %copy-start.8 = (s32[8,2]{0,1:T(2,128)S(1)}, s32[8,2]{0,1:T(2,128)}, u32[]{:S(2)}) copy-start(s32[8,2]{0,1:T(2,128)} %param.33) | copy-start | bytes 196
  50.7 50.2 %copy-start.9 = (f32[512]{0:T(512)S(1)}, f32[512]{0:T(512)}, u32[]{:S(2)}) copy-start(f32[512]{0:T(512)} %param.28) | copy-start | bytes 6148
  51.9 47.1 %collective-permute-start = (f32[512,2,256]{0,2,1:T(8,128)}, f32[512,2,256]{0,2,1:T(8,128)}, u32[]{:S(2)}, u32[]{:S(2)}) collective-permute-start(f32[512,2,256]{0,2,1:T(8,128)} %get-tuple-element.35), channel_id=1, source_target_pairs={{0,4},{4,8},{8,12},{12,16},{16,20},{20,24},{24,28},{28,0},{1,5},{5... | collective-permute-start | bytes 3145736 | tf_op jit(solution)/shard_map/ppermute | solution.py:18
  53.3 47.6 %collective-permute-start.1 = (f32[512,2,256]{0,2,1:T(8,128)S(1)}, f32[512,2,256]{0,2,1:T(8,128)}, u32[]{:S(2)}, u32[]{:S(2)}) collective-permute-start(f32[512,2,256]{0,2,1:T(8,128)S(1)} %get-tuple-element.36), channel_id=1, source_target_pairs={{4,0},{8,4},{12,8},{16,12},{20,16},{24,20},{28,24},{0,28},{5,1},{9... | collective-permute-start | bytes 3145736 | tf_op jit(solution)/shard_map/ppermute | solution.py:21
  132.9 7.6 %copy-start = (f32[512,8,256]{0,2,1:T(8,128)}, f32[512,8,256]{0,2,1:T(8,128)S(1)}, u32[]{:S(2)}) copy-start(f32[512,8,256]{0,2,1:T(8,128)S(1)} %fusion) | copy-start | bytes 12582916
  170.3 49.3 %copy-start.2 = (f32[512,8,256]{0,2,1:T(8,128)}, f32[512,8,256]{0,2,1:T(8,128)S(1)}, u32[]{:S(2)}) copy-start(f32[512,8,256]{0,2,1:T(8,128)S(1)} %bitcast_multiply_fusion) | copy-start | bytes 12582916
  170.5 46.8 %collective-permute-start.2 = (f32[512,2,256]{0,2,1:T(8,128)S(1)}, f32[512,2,256]{0,2,1:T(8,128)S(1)}, u32[]{:S(2)}, u32[]{:S(2)}) collective-permute-start(f32[512,2,256]{0,2,1:T(8,128)S(1)} %get-tuple-element.33), channel_id=1, source_target_pairs={{0,4},{4,8},{8,12},{12,16},{16,20},{20,24},{24,28},{28,0},{1,5},{5... | collective-permute-start | bytes 3145736 | tf_op jit(solution)/shard_map/ppermute | solution.py:18
  172.0 47.5 %collective-permute-start.3 = (f32[512,2,256]{0,2,1:T(8,128)S(1)}, f32[512,2,256]{0,2,1:T(8,128)S(1)}, u32[]{:S(2)}, u32[]{:S(2)}) collective-permute-start(f32[512,2,256]{0,2,1:T(8,128)S(1)} %get-tuple-element.34), channel_id=1, source_target_pairs={{4,0},{8,4},{12,8},{16,12},{20,16},{24,20},{28,24},{0,28},{5,1},{9... | collective-permute-start | bytes 3145736 | tf_op jit(solution)/shard_map/ppermute | solution.py:21
Sparse Core Ops, SparseCore 0:
  17.2 23.4 all-gather.2
  141.6 19.7 all-gather.4
